TPU v7x, 32 devices: a whole 2x2x4 slice. The times are simulated.
32 devices in a mesh: layer: 8 (over z, x), land: 4 (over y, core).
Axes of the slice: x: 2, y: 2, z: 4, core: 2. Of those that a mesh axis runs over, the one named last changes fastest.
Arguments:
- gradients: bfloat16 [960, 65536], P(None, ('layer', 'land')), may hold values from -6 to 6
- queries: bfloat16 [32, 65536], P(None, ('layer', 'land')), may hold values from -6 to 6
- landmarks: bfloat16 [1024, 65536], P(None, ('layer', 'land')), may hold values from -0.0234375 to 0.0234375
- whitening: bfloat16 [1024, 1024], P(None, 'land'), may hold values from -2.5 to 2.5
Outputs:
- scores: float32 [32, 960], P('land', 'layer')
All inputs are finite; a program needn't handle non-finite values.
Results may differ from a plain program's by a relative error of at most 0.023.
Values may be sent and summed in bfloat16 or wider, within the bound.
A program may use at most 128 MiB of HBM per device.

v0:
```python
import jax
import jax.numpy as jnp
from jax import lax
from jax.sharding import PartitionSpec as P

LANDMARKS = 1024


def contract_rows(rows, piece):
    return lax.dot_general(
        rows, piece, (((1,), (1,)), ((), ())), preferred_element_type=jnp.float32
    )


def make_folder(example_rows, query_rows, piece):
    return (contract_rows(example_rows, piece), contract_rows(query_rows, piece))


def local(gradients, queries, landmarks, whitening):
    n_layer = lax.axis_size("layer")
    n_land = lax.axis_size("land")
    width = gradients.shape[1]
    rows_each = gradients.shape[0] // (n_layer * n_land)
    query_each = queries.shape[0] // (n_layer * n_land)
    split_ex = gradients.reshape(n_layer, n_land, rows_each, width)
    split_qr = queries.reshape(n_layer, n_land, query_each, width)
    moved_ex, moved_qr = (
        lax.all_to_all(split_ex, "land", split_axis=1, concat_axis=3, tiled=True),
        lax.all_to_all(split_qr, "land", split_axis=1, concat_axis=3, tiled=True),
    )
    layer_rows = moved_ex.reshape(n_layer * rows_each, n_land * width)
    layer_query = moved_qr.reshape(n_layer * query_each, n_land * width)
    partial_ex, partial_qr = make_folder(
        layer_rows, layer_query, lax.all_gather(landmarks, "land", axis=1, tiled=True)
    )
    share_ex, share_qr = (
        lax.psum_scatter(
            partial_ex.astype(jnp.bfloat16), "layer", scatter_dimension=0, tiled=True
        ).astype(jnp.float32),
        lax.psum_scatter(
            partial_qr.astype(jnp.bfloat16), "layer", scatter_dimension=0, tiled=True
        ).astype(jnp.float32),
    )
    projected, query_proj = (
        lax.all_gather(share_ex.astype(jnp.bfloat16), "land", axis=0, tiled=True),
        lax.all_gather(share_qr.astype(jnp.bfloat16), "land", axis=0, tiled=True),
    )
    whitened = jnp.dot(projected, whitening, preferred_element_type=jnp.float32).astype(
        jnp.bfloat16
    )
    query_white = jnp.dot(query_proj, whitening, preferred_element_type=jnp.float32).astype(
        jnp.bfloat16
    )
    all_queries = lax.all_gather(query_white, "layer", axis=0, tiled=True)
    factor = LANDMARKS ** (-0.5)
    return lax.psum_scatter(
        (contract_rows(all_queries, whitened) * factor).astype(jnp.bfloat16),
        "land",
        scatter_dimension=0,
        tiled=True,
    ).astype(jnp.float32)


def solution(mesh):
    return jax.shard_map(
        local,
        mesh=mesh,
        in_specs=(
            P(None, ("layer", "land")),
            P(None, ("layer", "land")),
            P(None, ("layer", "land")),
            P(None, "land"),
        ),
        out_specs=P("land", "layer"),
        check_vma=False,
    )
```

profile of v0, /device:TPU:0, one launch (start us, length us, event | category | flops | bytes accessed | tf_op | source)
XLA Modules:
  0.0 296.0 jit_solution(8832669708729953579)
XLA Ops:
  6.5 0.0 copy-start
  6.5 0.0 all-gather.5.cloned.1.call-start
  6.5 0.7 all-gather.5.cloned.1.call-update
  7.3 5.0 %reshape.19 = bf16[8,4,30,2048]{3,2,1,0:T(8,128)(2,1)} reshape(bf16[960,2048]{1,0:T(8,128)(2,1)} %param.4) | data formatting | bytes 7864320 | tf_op jit(solution)/shard_map/reshape | solution.py:25
  12.3 6.4 %copy.9 = bf16[8,4,30,2048]{3,0,2,1:T(8,128)(2,1)} copy(bf16[8,4,30,2048]{3,2,1,0:T(8,128)(2,1)} %reshape.19) | data formatting | bytes 7864320 | tf_op jit(solution)/shard_map/reshape | solution.py:25
  18.7 0.0 copy-start.1
  18.7 0.0 copy-start.3
  18.7 0.0 copy-start.2
  18.7 5.1 %all-to-all-start.1 = ((bf16[8,4,30,2048]{3,0,2,1:T(8,128)(2,1)}), bf16[8,4,30,2048]{3,0,2,1:T(8,128)(2,1)}, u32[]{:S(2)}, u32[]{:S(2)}) async-start(bf16[8,4,30,2048]{3,0,2,1:T(8,128)(2,1)} %copy.9), calls=%async_computation.1 | async-start | bytes 7864320 | tf_op jit(solution)/shard_map/all_to_all | solution.py:28
  23.8 0.0 copy-done.1
  23.8 0.1 reshape.17
  23.9 0.7 copy.8
  24.6 0.0 copy-done.3
  24.6 0.6 dynamic-slice.4
  25.2 0.0 copy-done.2
  25.2 0.7 fusion.7
  27.1 85.5 %all-to-all-done.1 = bf16[8,4,30,2048]{3,0,2,1:T(8,128)(2,1)} async-done(((bf16[8,4,30,2048]{3,0,2,1:T(8,128)(2,1)}), bf16[8,4,30,2048]{3,0,2,1:T(8,128)(2,1)}, u32[]{:S(2)}, u32[]{:S(2)}) %all-to-all-start.1) | async-done | bytes 3932192 | tf_op jit(solution)/shard_map/all_to_all | solution.py:28
  112.6 3.5 %all-to-all-start = ((bf16[8,4,1,2048]{3,0,2,1:T(8,128)(2,1)}), bf16[8,4,1,2048]{3,0,2,1:T(8,128)(2,1)S(1)}, u32[]{:S(2)}, u32[]{:S(2)}) async-start(bf16[8,4,1,2048]{3,0,2,1:T(8,128)(2,1)} %copy.8), calls=%async_computation | async-start | bytes 262144 | tf_op jit(solution)/shard_map/all_to_all | solution.py:29
  116.1 5.1 %copy.10 = bf16[8,1,30,4,2048]{4,3,2,0,1:T(4,128)(2,1)S(1)} copy(bf16[8,1,30,4,2048]{4,0,2,3,1:T(8,128)(2,1)} %bitcast.4) | data formatting | bytes 7864320 | tf_op jit(solution)/shard_map/all_to_all | solution.py:28
  121.2 6.0 %copy.12 = bf16[30,8,4,2048]{3,1,2,0:T(8,128)(2,1)} copy(bf16[30,8,4,2048]{3,2,1,0:T(4,128)(2,1)S(1)} %bitcast.29) | data formatting | bytes 7864320
  127.2 33.9 %all-gather.5.cloned.1.call-done = bf16[1024,8192]{1,0:T(8,128)(2,1)} async-done(((bf16[1024,2048]{1,0:T(8,128)(2,1)}), bf16[1024,8192]{1,0:T(8,128)(2,1)}) %all-gather.5.cloned.1.call-update) | async-done | bytes 16777232 | tf_op jit(solution)/shard_map/all_gather | solution.py:34
  161.1 11.5 %convolution_convert_fusion = bf16[240,1024]{1,0:T(8,128)(2,1)S(1)} fusion(bf16[240,8192]{1,0:T(8,128)(2,1)} %bitcast.30, bf16[1024,8192]{1,0:T(8,128)(2,1)} %all-gather.5.cloned.1.call-done), kind=kOutput, calls=%fused_computation | convolution fusion | flops 4026777600 | bytes 21200896 | tf_op jit(solution)/shard_map/dot_general | solution.py:10
  172.6 25.3 %fusion = bf16[32,1024]{1,0:T(8,128)(2,1)S(1)} fusion(bf16[240,1024]{1,0:T(8,128)(2,1)S(1)} %convolution_convert_fusion), kind=kCustom, calls=%all-reduce-scatter | all-reduce-scatter fusion | flops 262145 | bytes 557568
  197.9 2.1 collective-permute-start
  200.0 0.0 all-to-all-done
  200.0 10.2 %convolution_convert_fusion.2 = bf16[8,1024]{1,0:T(8,128)(2,1)S(1)} fusion(bf16[8,8192]{1,0:T(8,128)(2,1)S(1)} %bitcast.31, bf16[1024,8192]{1,0:T(8,128)(2,1)} %all-gather.5.cloned.1.call-done), kind=kOutput, calls=%fused_computation.3 | convolution fusion | flops 134225920 | bytes 16924672 | tf_op jit(solution)/shard_map/dot_general | solution.py:10
  210.2 33.6 %all-reduce = bf16[8,1024]{1,0:T(8,128)(2,1)S(1)} all-reduce(bf16[8,1024]{1,0:T(8,128)(2,1)S(1)} %convolution_convert_fusion.2), channel_id=2, replica_groups=mesh['layer'=8,'land'=4] {'layer'}, use_global_device_ids=true, to_apply=%region_0.0.clone | all-reduce | flops 8192 | bytes 32768
  243.8 0.6 dynamic-slice_bitcast_fusion.1
  244.4 5.2 %all-gather = bf16[4,1,1024]{2,1,0:T(2,128)(2,1)S(1)} all-gather(bf16[1,1,1024]{2,1,0:T(2,128)(2,1)S(1)} %dynamic-slice_bitcast_fusion.1), channel_id=1, replica_groups=mesh['layer'=8,'land'=4] {'land'}, dimensions={0}, use_global_device_ids=true | all-gather | bytes 10240 | tf_op jit(solution)/shard_map/all_gather | solution.py:46
  249.6 0.0 copy-done
  249.6 0.2 fusion.4
  249.8 26.0 %all-gather.1 = bf16[8,4,256]{2,1,0:T(4,128)(2,1)S(1)} all-gather(bf16[1,4,256]{2,1,0:T(4,128)(2,1)S(1)} %fusion.4), channel_id=1, replica_groups=mesh['layer'=8,'land'=4] {'layer'}, dimensions={0}, use_global_device_ids=true | all-gather | bytes 18432 | tf_op jit(solution)/shard_map/all_gather | solution.py:54
  275.8 0.0 collective-permute-done
  275.8 0.2 concatenate
  276.1 5.8 %all-gather.2 = bf16[4,30,1024]{2,1,0:T(8,128)(2,1)S(1)} all-gather(bf16[1,30,1024]{2,1,0:T(8,128)(2,1)S(1)} %dynamic-slice_bitcast_fusion), channel_id=1, replica_groups=mesh['layer'=8,'land'=4] {'land'}, dimensions={0}, use_global_device_ids=true | all-gather | bytes 307200 | tf_op jit(solution)/shard_map/all_gather | solution.py:45
  281.9 0.1 reshape.26
  281.9 0.3 fusion.3
  282.3 6.2 %all-reduce.2 = bf16[32,120]{1,0:T(8,128)(2,1)S(1)} all-reduce(bf16[32,120]{1,0:T(8,128)(2,1)S(1)} %fusion.3), channel_id=4, replica_groups=mesh['layer'=8,'land'=4] {'land'}, use_global_device_ids=true, to_apply=%region_2.0.clone | all-reduce | flops 3840 | bytes 15360
  288.5 0.6 dynamic-slice_convert_fusion
  (3 shorter events, 0.1 us)
Async XLA Ops:
  6.5 243.1 %copy-start = (bf16[1024,256]{1,0:T(8,128)(2,1)S(1)}, bf16[1024,256]{1,0:T(8,128)(2,1)}, u32[]{:S(2)}) copy-start(bf16[1024,256]{1,0:T(8,128)(2,1)} %param.7) | copy-start | bytes 1572868
  6.5 154.6 %all-gather.5.cloned.1.call-start = ((), (), s32[]{:S(2)}) async-start(), calls=%async_computation.2 | async-start | bytes 20971520 | tf_op jit(solution)/shard_map/all_gather | solution.py:34
  18.7 5.1 %copy-start.1 = (bf16[32,2048]{1,0:T(8,128)(2,1)S(1)}, bf16[32,2048]{1,0:T(8,128)(2,1)}, u32[]{:S(2)}) copy-start(bf16[32,2048]{1,0:T(8,128)(2,1)} %param.5) | copy-start | bytes 393220
  18.7 6.0 %copy-start.3 = (u32[32]{0:T(128)S(1)}, u32[32]{0:T(128)}, u32[]{:S(2)}) copy-start(u32[32]{0:T(128)} %constant.12) | copy-start | bytes 388
  18.7 6.5 %copy-start.2 = (u32[32]{0:T(128)S(1)}, u32[32]{0:T(128)}, u32[]{:S(2)}) copy-start(u32[32]{0:T(128)} %constant.4) | copy-start | bytes 388
  18.7 93.9 %all-to-all-start.1 = ((bf16[8,4,30,2048]{3,0,2,1:T(8,128)(2,1)}), bf16[8,4,30,2048]{3,0,2,1:T(8,128)(2,1)}, u32[]{:S(2)}, u32[]{:S(2)}) async-start(bf16[8,4,30,2048]{3,0,2,1:T(8,128)(2,1)} %copy.9), calls=%async_computation.1 | async-start | bytes 7864320 | tf_op jit(solution)/shard_map/all_to_all | solution.py:28
  112.6 87.4 %all-to-all-start = ((bf16[8,4,1,2048]{3,0,2,1:T(8,128)(2,1)}), bf16[8,4,1,2048]{3,0,2,1:T(8,128)(2,1)S(1)}, u32[]{:S(2)}, u32[]{:S(2)}) async-start(bf16[8,4,1,2048]{3,0,2,1:T(8,128)(2,1)} %copy.8), calls=%async_computation | async-start | bytes 262144 | tf_op jit(solution)/shard_map/all_to_all | solution.py:29
  197.9 77.9 %collective-permute-start = (bf16[14,1024]{1,0:T(8,128)(2,1)S(1)}, bf16[14,1024]{1,0:T(8,128)(2,1)S(1)}, u32[]{:S(2)}, u32[]{:S(2)}) collective-permute-start(bf16[14,1024]{1,0:T(8,128)(2,1)S(1)} %slice), channel_id=1, source_target_pairs={{0,4},{4,8},{8,12},{12,16},{16,20},{20,24},{24,28},{1,5},{5,9},{9,... | collective-permute-start | bytes 86024
Sparse Core Ops, SparseCore 0:
  8.9 152.1 all-gather.4
where the time goes:
time: 297 us; the launch traced here: 296 us
  waiting for transfers between devices  120 us (40%)
  blocking collectives  102 us (34%)
  local copies, waits for them, and re-layouts  25.6 us (9%)
  matrix products  22.2 us (7%)
  between operations  14.8 us (5%)
  starting transfers between devices  10.7 us (4%)
    all_to_all x1, waiting for transfers between devices, local(): lax.all_to_all(split_ex, 'land', split_axis=1, concat_axis=3, tiled=True)  85.5 us
    unnamed x3, blocking collectives  65.1 us
    all_gather x1, waiting for transfers between devices, local(): lax.all_gather(landmarks, 'land', axis=1, tiled=True)  33.9 us
    all_gather x1, blocking collectives, local(): all_queries = lax.all_gather(query_white, 'layer', axis=0, tiled=True)  26 us
    dot_general x3, matrix products, contract_rows(): lax.dot_general(rows, piece, (((1,), (1,)), ((), ())), preferred_element_...  22 us
    reshape x2, local copies, waits for them, and re-layouts, local(): split_ex = gradients.reshape(n_layer, n_land, rows_each, width)  11.4 us
    unnamed x17, local copies, waits for them, and re-layouts  8.18 us
  transfers between devices with their start and end apart: 4, of which 2 were waited for; matrix products, arithmetic and copies ran while one was open for 24% of the time, Pallas kernels for 0%

commit v1 on v0

--- a/solution.py
+++ b/solution.py
@@ -2,6 +2,7 @@
 import jax.numpy as jnp
 from jax import lax
 from jax.sharding import PartitionSpec as P
+from jax.lax import axis_index, axis_size, ppermute
 
 LANDMARKS = 1024
 
@@ -51,7 +52,21 @@
     query_white = jnp.dot(query_proj, whitening, preferred_element_type=jnp.float32).astype(
         jnp.bfloat16
     )
-    all_queries = lax.all_gather(query_white, "layer", axis=0, tiled=True)
+
+    def _view_cubes(matrix, device_axis):
+        slots = axis_size(device_axis)
+        x_now = sorted(((hop_no, (hop_no + 1) % slots) for hop_no in range(slots)))
+        y1 = matrix
+        pages = [y1]
+        for pp in range(1, slots):
+            y1 = ppermute(y1, device_axis, perm=x_now)
+            pages.insert(0, y1)
+        answer = jnp.concatenate(pages, 0)
+        far_arr = axis_index(device_axis)
+        opened = far_arr + 1
+        return jnp.roll(answer, opened * matrix.shape[0], axis=0)
+
+    all_queries = _view_cubes(query_white, "layer")
     factor = LANDMARKS ** (-0.5)
     return lax.psum_scatter(
         (contract_rows(all_queries, whitened) * factor).astype(jnp.bfloat16),

time: 297 us -> 315 us (1.061)
  waiting for transfers between devices: 120 us -> 164 us
  blocking collectives: 102 us -> 76.1 us
    ppermute x0 -> x7, waiting for transfers between devices: none -> 42 us  [_view_cubes(): y1 = ppermute(y1, device_axis, perm=x_now)]
    all_gather x1 -> x0, blocking collectives: 26 us -> none  [local(): all_queries = lax.all_gather(query_white, 'layer', axis=0, tiled=True)]
    unnamed x17 -> x16, local copies, waits for them, and re-layouts: 8.18 us -> 8.2 us
  transfers between devices with their start and end apart: 4 -> 11, of which waited for: 2 -> 9; matrix products, arithmetic and copies ran while one was open for 24% -> 23% of each run, Pallas kernels for 0% -> 0%
where the time goes in v1:
time: 315 us; the launch traced here: 314 us
  waiting for transfers between devices  164 us (52%)
  blocking collectives  76.1 us (24%)
  local copies, waits for them, and re-layouts  25.8 us (8%)
  matrix products  22.2 us (7%)
  between operations  14.9 us (5%)
  starting transfers between devices  10.7 us (3%)
    all_to_all x1, waiting for transfers between devices, local(): lax.all_to_all(split_ex, 'land', split_axis=1, concat_axis=3, tiled=True)  87.3 us
    unnamed x3, blocking collectives  65.1 us
    ppermute x7, waiting for transfers between devices, _view_cubes(): y1 = ppermute(y1, device_axis, perm=x_now)  42 us
    all_gather x1, waiting for transfers between devices, local(): lax.all_gather(landmarks, 'land', axis=1, tiled=True)  33.9 us
    dot_general x3, matrix products, contract_rows(): lax.dot_general(rows, piece, (((1,), (1,)), ((), ())), preferred_element_...  22 us
    reshape x2, local copies, waits for them, and re-layouts, local(): split_ex = gradients.reshape(n_layer, n_land, rows_each, width)  11.4 us
    unnamed x16, local copies, waits for them, and re-layouts  8.2 us
  transfers between devices with their start and end apart: 11, of which 9 were waited for; matrix products, arithmetic and copies ran while one was open for 23% of the time, Pallas kernels for 0%

profile of v1, /device:TPU:0, one launch (start us, length us, event | category | flops | bytes accessed | tf_op | source)
XLA Modules:
  0.0 314.2 jit_solution(12606751874489329123)
XLA Ops:
  6.5 0.0 copy-start
  6.5 0.0 all-gather.4.cloned.1.call-start
  6.5 0.7 all-gather.4.cloned.1.call-update
  7.3 5.1 %reshape.19 = bf16[8,4,30,2048]{3,2,1,0:T(8,128)(2,1)} reshape(bf16[960,2048]{1,0:T(8,128)(2,1)} %param.4) | data formatting | bytes 7864320 | tf_op jit(solution)/shard_map/reshape | solution.py:26
  12.3 6.4 %copy.9 = bf16[8,4,30,2048]{3,0,2,1:T(8,128)(2,1)} copy(bf16[8,4,30,2048]{3,2,1,0:T(8,128)(2,1)} %reshape.19) | data formatting | bytes 7864320 | tf_op jit(solution)/shard_map/reshape | solution.py:26
  18.7 5.1 %all-to-all-start.1 = ((bf16[8,4,30,2048]{3,0,2,1:T(8,128)(2,1)}), bf16[8,4,30,2048]{3,0,2,1:T(8,128)(2,1)}, u32[]{:S(2)}, u32[]{:S(2)}) async-start(bf16[8,4,30,2048]{3,0,2,1:T(8,128)(2,1)} %copy.9), calls=%async_computation.1 | async-start | bytes 7864320 | tf_op jit(solution)/shard_map/all_to_all | solution.py:29
  23.8 0.0 copy-done.1
  23.8 0.1 reshape.17
  23.9 0.7 copy.8
  24.6 0.7 fusion.8
  25.3 87.3 %all-to-all-done.1 = bf16[8,4,30,2048]{3,0,2,1:T(8,128)(2,1)} async-done(((bf16[8,4,30,2048]{3,0,2,1:T(8,128)(2,1)}), bf16[8,4,30,2048]{3,0,2,1:T(8,128)(2,1)}, u32[]{:S(2)}, u32[]{:S(2)}) %all-to-all-start.1) | async-done | bytes 3932192 | tf_op jit(solution)/shard_map/all_to_all | solution.py:29
  112.6 3.5 %all-to-all-start = ((bf16[8,4,1,2048]{3,0,2,1:T(8,128)(2,1)}), bf16[8,4,1,2048]{3,0,2,1:T(8,128)(2,1)S(1)}, u32[]{:S(2)}, u32[]{:S(2)}) async-start(bf16[8,4,1,2048]{3,0,2,1:T(8,128)(2,1)} %copy.8), calls=%async_computation | async-start | bytes 262144 | tf_op jit(solution)/shard_map/all_to_all | solution.py:30
  116.1 5.1 %copy.10 = bf16[8,1,30,4,2048]{4,3,2,0,1:T(4,128)(2,1)S(1)} copy(bf16[8,1,30,4,2048]{4,0,2,3,1:T(8,128)(2,1)} %bitcast.3) | data formatting | bytes 7864320 | tf_op jit(solution)/shard_map/all_to_all | solution.py:29
  121.3 6.0 %copy.12 = bf16[30,8,4,2048]{3,1,2,0:T(8,128)(2,1)} copy(bf16[30,8,4,2048]{3,2,1,0:T(4,128)(2,1)S(1)} %bitcast.26) | data formatting | bytes 7864320
  127.2 33.9 %all-gather.4.cloned.1.call-done = bf16[1024,8192]{1,0:T(8,128)(2,1)} async-done(((bf16[1024,2048]{1,0:T(8,128)(2,1)}), bf16[1024,8192]{1,0:T(8,128)(2,1)}) %all-gather.4.cloned.1.call-update) | async-done | bytes 16777232 | tf_op jit(solution)/shard_map/all_gather | solution.py:35
  161.1 11.5 %convolution_convert_fusion = bf16[240,1024]{1,0:T(8,128)(2,1)S(1)} fusion(bf16[240,8192]{1,0:T(8,128)(2,1)} %bitcast.27, bf16[1024,8192]{1,0:T(8,128)(2,1)} %all-gather.4.cloned.1.call-done), kind=kOutput, calls=%fused_computation | convolution fusion | flops 4026777600 | bytes 21200896 | tf_op jit(solution)/shard_map/dot_general | solution.py:11
  172.6 25.3 %fusion = bf16[32,1024]{1,0:T(8,128)(2,1)S(1)} fusion(bf16[240,1024]{1,0:T(8,128)(2,1)S(1)} %convolution_convert_fusion), kind=kCustom, calls=%all-reduce-scatter | all-reduce-scatter fusion | flops 262145 | bytes 557568
  197.9 2.1 collective-permute-start.7
  200.0 0.0 all-to-all-done
  200.0 0.0 copy-start.3
  200.0 10.2 %convolution_convert_fusion.2 = bf16[8,1024]{1,0:T(8,128)(2,1)S(1)} fusion(bf16[8,8192]{1,0:T(8,128)(2,1)S(1)} %bitcast.28, bf16[1024,8192]{1,0:T(8,128)(2,1)} %all-gather.4.cloned.1.call-done), kind=kOutput, calls=%fused_computation.3 | convolution fusion | flops 134225920 | bytes 16924672 | tf_op jit(solution)/shard_map/dot_general | solution.py:11
  210.2 33.6 %all-reduce = bf16[8,1024]{1,0:T(8,128)(2,1)S(1)} all-reduce(bf16[8,1024]{1,0:T(8,128)(2,1)S(1)} %convolution_convert_fusion.2), channel_id=2, replica_groups=mesh['layer'=8,'land'=4] {'layer'}, use_global_device_ids=true, to_apply=%region_0.0.clone | all-reduce | flops 8192 | bytes 32768
  243.8 0.7 dynamic-slice_bitcast_fusion.1
  244.5 5.2 %all-gather = bf16[4,1,1024]{2,1,0:T(2,128)(2,1)S(1)} all-gather(bf16[1,1,1024]{2,1,0:T(2,128)(2,1)S(1)} %dynamic-slice_bitcast_fusion.1), channel_id=1, replica_groups=mesh['layer'=8,'land'=4] {'land'}, dimensions={0}, use_global_device_ids=true | all-gather | bytes 10240 | tf_op jit(solution)/shard_map/all_gather | solution.py:47
  249.7 0.2 convolution_convert_fusion.3
  249.8 0.0 collective-permute-start
  249.8 6.3 %collective-permute-done = bf16[4,256]{1,0:T(4,128)(2,1)S(1)} collective-permute-done((bf16[4,256]{1,0:T(4,128)(2,1)S(1)}, bf16[4,256]{1,0:T(4,128)(2,1)S(1)}, u32[]{:S(2)}, u32[]{:S(2)}) %collective-permute-start) | collective-permute-done | bytes 2080 | tf_op jit(solution)/shard_map/ppermute | solution.py:62
  256.1 0.0 collective-permute-start.1
  256.1 6.3 %collective-permute-done.1 = bf16[4,256]{1,0:T(4,128)(2,1)S(1)} collective-permute-done((bf16[4,256]{1,0:T(4,128)(2,1)S(1)}, bf16[4,256]{1,0:T(4,128)(2,1)S(1)}, u32[]{:S(2)}, u32[]{:S(2)}) %collective-permute-start.1) | collective-permute-done | bytes 2080 | tf_op jit(solution)/shard_map/ppermute | solution.py:62
  262.4 0.0 collective-permute-start.2
  262.4 6.3 %collective-permute-done.2 = bf16[4,256]{1,0:T(4,128)(2,1)S(1)} collective-permute-done((bf16[4,256]{1,0:T(4,128)(2,1)S(1)}, bf16[4,256]{1,0:T(4,128)(2,1)S(1)}, u32[]{:S(2)}, u32[]{:S(2)}) %collective-permute-start.2) | collective-permute-done | bytes 2080 | tf_op jit(solution)/shard_map/ppermute | solution.py:62
  268.7 0.0 collective-permute-start.3
  268.7 6.3 %collective-permute-done.3 = bf16[4,256]{1,0:T(4,128)(2,1)S(1)} collective-permute-done((bf16[4,256]{1,0:T(4,128)(2,1)S(1)}, bf16[4,256]{1,0:T(4,128)(2,1)S(1)}, u32[]{:S(2)}, u32[]{:S(2)}) %collective-permute-start.3) | collective-permute-done | bytes 2080 | tf_op jit(solution)/shard_map/ppermute | solution.py:62
  275.0 0.0 collective-permute-start.4
  275.0 6.3 %collective-permute-done.4 = bf16[4,256]{1,0:T(4,128)(2,1)S(1)} collective-permute-done((bf16[4,256]{1,0:T(4,128)(2,1)S(1)}, bf16[4,256]{1,0:T(4,128)(2,1)S(1)}, u32[]{:S(2)}, u32[]{:S(2)}) %collective-permute-start.4) | collective-permute-done | bytes 2080 | tf_op jit(solution)/shard_map/ppermute | solution.py:62
  281.3 0.0 collective-permute-start.5
  281.3 6.3 %collective-permute-done.5 = bf16[4,256]{1,0:T(4,128)(2,1)S(1)} collective-permute-done((bf16[4,256]{1,0:T(4,128)(2,1)S(1)}, bf16[4,256]{1,0:T(4,128)(2,1)S(1)}, u32[]{:S(2)}, u32[]{:S(2)}) %collective-permute-start.5) | collective-permute-done | bytes 2080 | tf_op jit(solution)/shard_map/ppermute | solution.py:62
  287.6 0.0 collective-permute-start.6
  287.6 0.6 dynamic-slice.4
  289.5 4.4 %collective-permute-done.6 = bf16[4,256]{1,0:T(4,128)(2,1)S(1)} collective-permute-done((bf16[4,256]{1,0:T(4,128)(2,1)S(1)}, bf16[4,256]{1,0:T(4,128)(2,1)S(1)}, u32[]{:S(2)}, u32[]{:S(2)}) %collective-permute-start.6) | collective-permute-done | bytes 2080 | tf_op jit(solution)/shard_map/ppermute | solution.py:62
  293.8 0.2 concatenate.6
  294.0 0.0 collective-permute-done.7
  294.0 0.2 concatenate.7
  294.3 5.8 %all-gather.1 = bf16[4,30,1024]{2,1,0:T(8,128)(2,1)S(1)} all-gather(bf16[1,30,1024]{2,1,0:T(8,128)(2,1)S(1)} %dynamic-slice_bitcast_fusion), channel_id=1, replica_groups=mesh['layer'=8,'land'=4] {'land'}, dimensions={0}, use_global_device_ids=true | all-gather | bytes 307200 | tf_op jit(solution)/shard_map/all_gather | solution.py:46
  300.1 0.1 reshape.24
  300.1 0.4 fusion.3
  300.5 6.2 %all-reduce.2 = bf16[32,120]{1,0:T(8,128)(2,1)S(1)} all-reduce(bf16[32,120]{1,0:T(8,128)(2,1)S(1)} %fusion.3), channel_id=4, replica_groups=mesh['layer'=8,'land'=4] {'land'}, use_global_device_ids=true, to_apply=%region_2.3.clone | all-reduce | flops 3840 | bytes 15360
  306.7 0.6 dynamic-slice_convert_fusion
  (7 shorter events, 0.0 us)
Async XLA Ops:
  6.5 243.1 %copy-start = (bf16[1024,256]{1,0:T(8,128)(2,1)S(1)}, bf16[1024,256]{1,0:T(8,128)(2,1)}, u32[]{:S(2)}) copy-start(bf16[1024,256]{1,0:T(8,128)(2,1)} %param.7) | copy-start | bytes 1572868
  6.5 154.6 %all-gather.4.cloned.1.call-start = ((), (), s32[]{:S(2)}) async-start(), calls=%async_computation.2 | async-start | bytes 20971520 | tf_op jit(solution)/shard_map/all_gather | solution.py:35
  18.7 5.1 %copy-start.1 = (bf16[32,2048]{1,0:T(8,128)(2,1)S(1)}, bf16[32,2048]{1,0:T(8,128)(2,1)}, u32[]{:S(2)}) copy-start(bf16[32,2048]{1,0:T(8,128)(2,1)} %param.5) | copy-start | bytes 393220
  18.7 5.9 %copy-start.2 = (u32[32]{0:T(128)S(1)}, u32[32]{0:T(128)}, u32[]{:S(2)}) copy-start(u32[32]{0:T(128)} %constant.36) | copy-start | bytes 388
  18.7 93.9 %all-to-all-start.1 = ((bf16[8,4,30,2048]{3,0,2,1:T(8,128)(2,1)}), bf16[8,4,30,2048]{3,0,2,1:T(8,128)(2,1)}, u32[]{:S(2)}, u32[]{:S(2)}) async-start(bf16[8,4,30,2048]{3,0,2,1:T(8,128)(2,1)} %copy.9), calls=%async_computation.1 | async-start | bytes 7864320 | tf_op jit(solution)/shard_map/all_to_all | solution.py:29
  112.6 87.4 %all-to-all-start = ((bf16[8,4,1,2048]{3,0,2,1:T(8,128)(2,1)}), bf16[8,4,1,2048]{3,0,2,1:T(8,128)(2,1)S(1)}, u32[]{:S(2)}, u32[]{:S(2)}) async-start(bf16[8,4,1,2048]{3,0,2,1:T(8,128)(2,1)} %copy.8), calls=%async_computation | async-start | bytes 262144 | tf_op jit(solution)/shard_map/all_to_all | solution.py:30
  197.9 96.1 %collective-permute-start.7 = (bf16[14,1024]{1,0:T(8,128)(2,1)S(1)}, bf16[14,1024]{1,0:T(8,128)(2,1)S(1)}, u32[]{:S(2)}, u32[]{:S(2)}) collective-permute-start(bf16[14,1024]{1,0:T(8,128)(2,1)S(1)} %slice), channel_id=1, source_target_pairs={{0,4},{4,8},{8,12},{12,16},{16,20},{20,24},{24,28},{1,5},{5,9},{9,... | collective-permute-start | bytes 86024
  200.0 87.5 %copy-start.3 = (u32[32]{0:T(128)S(1)}, u32[32]{0:T(128)}, u32[]{:S(2)}) copy-start(u32[32]{0:T(128)} %constant.44) | copy-start | bytes 388
  249.8 6.3 %collective-permute-start = (bf16[4,256]{1,0:T(4,128)(2,1)S(1)}, bf16[4,256]{1,0:T(4,128)(2,1)S(1)}, u32[]{:S(2)}, u32[]{:S(2)}) collective-permute-start(bf16[4,256]{1,0:T(4,128)(2,1)S(1)} %convolution_convert_fusion.3), channel_id=1, source_target_pairs={{0,4},{4,8},{8,12},{12,16},{16,20},{20,24},{24,28},{28,0},{1,5},{5... | collective-permute-start | bytes 6152 | tf_op jit(solution)/shard_map/ppermute | solution.py:62
  256.1 6.3 %collective-permute-start.1 = (bf16[4,256]{1,0:T(4,128)(2,1)S(1)}, bf16[4,256]{1,0:T(4,128)(2,1)S(1)}, u32[]{:S(2)}, u32[]{:S(2)}) collective-permute-start(bf16[4,256]{1,0:T(4,128)(2,1)S(1)} %collective-permute-done), channel_id=1, source_target_pairs={{0,4},{4,8},{8,12},{12,16},{16,20},{20,24},{24,28},{28,0},{1,5},{5... | collective-permute-start | bytes 6152 | tf_op jit(solution)/shard_map/ppermute | solution.py:62
  262.4 6.3 %collective-permute-start.2 = (bf16[4,256]{1,0:T(4,128)(2,1)S(1)}, bf16[4,256]{1,0:T(4,128)(2,1)S(1)}, u32[]{:S(2)}, u32[]{:S(2)}) collective-permute-start(bf16[4,256]{1,0:T(4,128)(2,1)S(1)} %collective-permute-done.1), channel_id=1, source_target_pairs={{0,4},{4,8},{8,12},{12,16},{16,20},{20,24},{24,28},{28,0},{1,5},{5... | collective-permute-start | bytes 6152 | tf_op jit(solution)/shard_map/ppermute | solution.py:62
  268.7 6.3 %collective-permute-start.3 = (bf16[4,256]{1,0:T(4,128)(2,1)S(1)}, bf16[4,256]{1,0:T(4,128)(2,1)S(1)}, u32[]{:S(2)}, u32[]{:S(2)}) collective-permute-start(bf16[4,256]{1,0:T(4,128)(2,1)S(1)} %collective-permute-done.2), channel_id=1, source_target_pairs={{0,4},{4,8},{8,12},{12,16},{16,20},{20,24},{24,28},{28,0},{1,5},{5... | collective-permute-start | bytes 6152 | tf_op jit(solution)/shard_map/ppermute | solution.py:62
  275.0 6.3 %collective-permute-start.4 = (bf16[4,256]{1,0:T(4,128)(2,1)S(1)}, bf16[4,256]{1,0:T(4,128)(2,1)S(1)}, u32[]{:S(2)}, u32[]{:S(2)}) collective-permute-start(bf16[4,256]{1,0:T(4,128)(2,1)S(1)} %collective-permute-done.3), channel_id=1, source_target_pairs={{0,4},{4,8},{8,12},{12,16},{16,20},{20,24},{24,28},{28,0},{1,5},{5... | collective-permute-start | bytes 6152 | tf_op jit(solution)/shard_map/ppermute | solution.py:62
  281.3 6.3 %collective-permute-start.5 = (bf16[4,256]{1,0:T(4,128)(2,1)S(1)}, bf16[4,256]{1,0:T(4,128)(2,1)S(1)}, u32[]{:S(2)}, u32[]{:S(2)}) collective-permute-start(bf16[4,256]{1,0:T(4,128)(2,1)S(1)} %collective-permute-done.4), channel_id=1, source_target_pairs={{0,4},{4,8},{8,12},{12,16},{16,20},{20,24},{24,28},{28,0},{1,5},{5... | collective-permute-start | bytes 6152 | tf_op jit(solution)/shard_map/ppermute | solution.py:62
  287.6 6.3 %collective-permute-start.6 = (bf16[4,256]{1,0:T(4,128)(2,1)S(1)}, bf16[4,256]{1,0:T(4,128)(2,1)S(1)}, u32[]{:S(2)}, u32[]{:S(2)}) collective-permute-start(bf16[4,256]{1,0:T(4,128)(2,1)S(1)} %collective-permute-done.5), channel_id=1, source_target_pairs={{0,4},{4,8},{8,12},{12,16},{16,20},{20,24},{24,28},{28,0},{1,5},{5... | collective-permute-start | bytes 6152 | tf_op jit(solution)/shard_map/ppermute | solution.py:62
Sparse Core Ops, SparseCore 0:
  8.9 152.1 all-gather.3
